TPU v7x, 128 devices: a whole 4x4x4 slice. The times are simulated.
128 devices in a mesh: row: 8 (over x_hi, y), col: 16 (over z, x_lo, core).
Axes of the slice: x: 4 (x_hi: 2, x_lo: 2; x = x_hi * 2 + x_lo), y: 4, z: 4, core: 2. Of those that a mesh axis runs over, the one named last changes fastest.
Arguments:
- doubles: float32 [32, 32, 192, 192], P(None, None, 'row', 'col'), may hold values from -6 to 6
- cycle_inter: float32 [6144, 6144], P('row', 'col'), may hold values from -0.078125 to 0.078125
Outputs:
- cycle_term: float32 [6144, 6144], P('row', 'col')
All inputs are finite; a program needn't handle non-finite values.
Results may differ from a plain program's by a relative error of at most 0.00007.
Values sent between devices are 32-bit elements; how exact they have to be, the bound alone decides.
A program may use at most 192 MiB of HBM per device.

v0:
```python
import jax
import jax.numpy as jnp
from jax import lax
from jax.sharding import PartitionSpec as P

V = 192


def body(doubles, cycle_inter):
    moved = lax.all_to_all(
        lax.all_to_all(doubles, "row", split_axis=0, concat_axis=2, tiled=True),
        "col",
        split_axis=1,
        concat_axis=3,
        tiled=True,
    )
    kloc = moved.shape[0]
    jloc = moved.shape[1]
    local_panel = jnp.transpose(moved, (0, 2, 1, 3)).reshape(kloc * V, jloc * V)
    amp_panel = lax.all_gather(local_panel, "row", axis=0, tiled=True)
    return jnp.dot(
        lax.all_gather(cycle_inter, "col", axis=1, tiled=True),
        amp_panel,
        precision=lax.Precision.HIGHEST,
        preferred_element_type=jnp.float32,
    )


def solution(mesh):
    placed = (P(None, None, "row", "col"), P("row", "col"))
    return jax.shard_map(
        body, mesh=mesh, in_specs=placed, out_specs=P("row", "col"), check_vma=False
    )
```

profile of v0, /device:TPU:1, one launch (start us, length us, event | category | flops | bytes accessed | tf_op | source)
XLA Modules:
  0.0 342.0 jit_solution(5271880841259820000)
XLA Ops:
  6.5 0.0 all-gather.5.cloned.1.call-start
  6.5 4.2 %reshape.4 = f32[8,1,36864]{2,1,0:T(1,128)S(1)} reshape(f32[32,12,24,32]{3,2,1,0:T(8,128)} %bitcast.20) | data formatting | bytes 2359296
  10.7 24.7 %all_to_all.36 = f32[8,1,36864]{2,1,0:T(1,128)S(1)} all-to-all(f32[8,1,36864]{2,1,0:T(1,128)S(1)} %reshape.4), channel_id=1, replica_groups=mesh['row'=8,'col'=16] {'row'}, dimensions={0} | all-to-all | bytes 2359296 | tf_op jit(solution)/shard_map/all_to_all | solution.py:11
  35.4 0.5 broadcast
  35.9 3.4 %reduce = f32[8,36864]{1,0:T(8,128)S(1)} reduce(f32[8,1,36864]{2,1,0:T(1,128)S(1)} %all_to_all.36, f32[]{:T(128)} %broadcast), dimensions={1}, to_apply=%all_to_all.26.reduce_sub_computation | reduce | bytes 2359300 | tf_op jit(solution)/shard_map/all_to_all | solution.py:11
  39.4 3.8 %reshape.5 = f32[32,12,24,32]{3,2,1,0:T(8,128)} reshape(f32[8,36864]{1,0:T(8,128)S(1)} %reduce) | data formatting | bytes 2359296
  43.1 6.3 %copy.10 = f32[8,4,32,24,12]{3,0,2,4,1:T(8,128)} copy(f32[8,4,32,24,12]{2,3,4,1,0:T(8,128)} %bitcast.17) | data formatting | bytes 2359296 | tf_op jit(solution)/shard_map/all_to_all | solution.py:11
  49.4 4.2 %all_to_all.29 = f32[4,32,192,12]{2,1,3,0:T(8,128)S(1)} reshape(f32[4,32,8,24,12]{3,2,1,4,0:T(8,128)} %bitcast.16) | data formatting | bytes 2359296 | tf_op jit(solution)/shard_map/all_to_all | solution.py:11
  53.6 1.0 copy.11
  54.7 28.3 %all_to_all.37 = f32[4,32,192,12]{2,0,3,1:T(4,128)S(1)} all-to-all(f32[4,32,192,12]{2,0,3,1:T(4,128)S(1)} %copy.11), channel_id=1, replica_groups=mesh['row'=8,'col'=16] {'col'}, dimensions={1} | all-to-all | bytes 2359296 | tf_op jit(solution)/shard_map/all_to_all | solution.py:10
  83.0 1.2 copy.12
  84.2 1.0 copy.13
  85.2 2.3 reshape.3
  87.5 0.0 all-gather.5.cloned.1.call-update
  87.5 0.2 all-gather.3.cloned.1.call-start
  87.7 0.5 all-gather.3.cloned.1.call-update
  88.3 110.7 %all-gather.5.cloned.1.call-done = f32[6144,384]{1,0:T(8,128)} async-done(((f32[768,384]{1,0:T(8,128)}), f32[6144,384]{1,0:T(8,128)}) %all-gather.5.cloned.1.call-update) | async-done | bytes 9437200 | tf_op jit(solution)/shard_map/all_gather | solution.py:20
  198.9 102.2 %all-gather.3.cloned.1.call-done = f32[768,6144]{1,0:T(8,128)} async-done(((f32[768,384]{1,0:T(8,128)}), f32[768,6144]{1,0:T(8,128)}) %all-gather.3.cloned.1.call-update) | async-done | bytes 18874384 | tf_op jit(solution)/shard_map/all_gather | solution.py:22
  301.1 34.1 %fusion = f32[768,384]{1,0:T(8,128)} fusion(f32[768,6144]{1,0:T(8,128)} %all-gather.3.cloned.1.call-done, f32[6144,384]{1,0:T(8,128)} %all-gather.5.cloned.1.call-done), kind=kOutput, calls=%fused_computation | convolution fusion | flops 21743271936 | bytes 29491200 | tf_op jit(solution)/shard_map/dot_general | solution.py:21
Async XLA Ops:
  6.5 192.4 %all-gather.5.cloned.1.call-start = ((), (), s32[]{:S(2)}) async-start(), calls=%async_computation.3 | async-start | bytes 10616832 | tf_op jit(solution)/shard_map/all_gather | solution.py:20
  87.5 213.6 %all-gather.3.cloned.1.call-start = ((), (), s32[]{:S(2)}) async-start(), calls=%async_computation.2 | async-start | bytes 20054016 | tf_op jit(solution)/shard_map/all_gather | solution.py:22
Sparse Core Ops, SparseCore 0:
  87.6 111.2 all-gather.4
  200.6 100.5 all-gather.2
where the time goes:
time: 342 us
  waiting for transfers between devices  213 us (62%)
  blocking collectives  53 us (15%)
  matrix products  34.1 us (10%)
  local copies, waits for them, and re-layouts  24.5 us (7%)
  between operations  13.4 us (4%)
  other arithmetic  3.45 us (1%)
    all_gather x1, waiting for transfers between devices, body(): amp_panel = lax.all_gather(local_panel, 'row', axis=0, tiled=True)  111 us
    all_gather x1, waiting for transfers between devices, body(): lax.all_gather(cycle_inter, 'col', axis=1, tiled=True)  102 us
    dot_general x1, matrix products, body(): jnp.dot(lax.all_gather(cycle_inter, 'col', axis=1, tiled=True), amp_panel...  34.1 us
    all_to_all x1, blocking collectives, body(): lax.all_to_all(lax.all_to_all(doubles, 'row', split_axis=0, concat_axis=2...  28.3 us
    all_to_all x1, blocking collectives, body(): lax.all_to_all(doubles, 'row', split_axis=0, concat_axis=2, tiled=True)  24.7 us
    all_to_all x4, local copies, waits for them, and re-layouts, body(): lax.all_to_all(doubles, 'row', split_axis=0, concat_axis=2, tiled=True)  12 us
    unnamed x2, local copies, waits for them, and re-layouts  7.95 us
  transfers between devices with their start and end apart: 2, of which 2 were waited for; matrix products, arithmetic and copies ran while one was open for 0% of the time, Pallas kernels for 0%

commit v1 on v0

--- a/solution.py
+++ b/solution.py
@@ -17,7 +17,8 @@
     kloc = moved.shape[0]
     jloc = moved.shape[1]
     local_panel = jnp.transpose(moved, (0, 2, 1, 3)).reshape(kloc * V, jloc * V)
-    amp_panel = lax.all_gather(local_panel, "row", axis=0, tiled=True)
+    outgoing = jnp.stack([local_panel] * lax.axis_size("row"))
+    amp_panel = jnp.concatenate(lax.all_to_all(outgoing, "row", 0, 0), axis=0)
     return jnp.dot(
         lax.all_gather(cycle_inter, "col", axis=1, tiled=True),
         amp_panel,

time: 342 us -> 285 us (0.83)
  waiting for transfers between devices: 213 us -> 0.71 us
  blocking collectives: 53 us -> 208 us
    all_to_all x0 -> x1, blocking collectives: none -> 126 us  [body(): amp_panel = jnp.concatenate(lax.all_to_all(outgoing, 'row', 0, 0), axis=0)]
    all_gather x1 -> x0, waiting for transfers between devices: 111 us -> none  [body(): amp_panel = lax.all_gather(local_panel, 'row', axis=0, tiled=True)]
    all_gather x1, waiting for transfers between devices: 102 us -> 0.01 us  [body(): lax.all_gather(cycle_inter, 'col', axis=1, tiled=True)]
    all_to_all x1, blocking collectives: 28.3 us -> 49.3 us  [body(): lax.all_to_all(lax.all_to_all(doubles, 'row', split_axis=0, concat_axis=2...]
    all_to_all x1, blocking collectives: 24.7 us -> 33.5 us  [body(): lax.all_to_all(doubles, 'row', split_axis=0, concat_axis=2, tiled=True)]
  transfers between devices with their start and end apart: 2 -> 1, of which waited for: 2 -> 0; matrix products, arithmetic and copies ran while one was open for 0% -> 8% of each run, Pallas kernels for 0% -> 0%
where the time goes in v1:
time: 285 us; the launch traced here: 284 us
  blocking collectives  208 us (73%)
  matrix products  34.1 us (12%)
  local copies, waits for them, and re-layouts  24.1 us (8%)
  between operations  13.5 us (5%)
  other arithmetic  3.45 us (1%)
    all_to_all x1, blocking collectives, body(): amp_panel = jnp.concatenate(lax.all_to_all(outgoing, 'row', 0, 0), axis=0)  126 us
    all_to_all x1, blocking collectives, body(): lax.all_to_all(lax.all_to_all(doubles, 'row', split_axis=0, concat_axis=2...  49.3 us
    dot_general x1, matrix products, body(): jnp.dot(lax.all_gather(cycle_inter, 'col', axis=1, tiled=True), amp_panel...  34.1 us
    all_to_all x1, blocking collectives, body(): lax.all_to_all(doubles, 'row', split_axis=0, concat_axis=2, tiled=True)  33.5 us
    all_to_all x4, local copies, waits for them, and re-layouts, body(): lax.all_to_all(doubles, 'row', split_axis=0, concat_axis=2, tiled=True)  12.1 us
    unnamed x2, local copies, waits for them, and re-layouts  7.9 us
  transfers between devices with their start and end apart: 1, of which 0 were waited for; matrix products, arithmetic and copies ran while one was open for 8% of the time, Pallas kernels for 0%

profile of v1, /device:TPU:1, one launch (start us, length us, event | category | flops | bytes accessed | tf_op | source)
XLA Modules:
  0.0 284.3 jit_solution(9649727443030879012)
XLA Ops:
  6.5 0.0 all-gather.2.cloned.1.call-start
  6.5 0.7 all-gather.2.cloned.1.call-update
  7.3 4.2 %reshape.6 = f32[8,1,36864]{2,1,0:T(1,128)S(1)} reshape(f32[32,12,24,32]{3,2,1,0:T(8,128)} %bitcast.22) | data formatting | bytes 2359296
  11.5 33.5 %all_to_all.41 = f32[8,1,36864]{2,1,0:T(1,128)S(1)} all-to-all(f32[8,1,36864]{2,1,0:T(1,128)S(1)} %reshape.6), channel_id=1, replica_groups=mesh['row'=8,'col'=16] {'row'}, dimensions={0} | all-to-all | bytes 2359296 | tf_op jit(solution)/shard_map/all_to_all | solution.py:11
  45.0 0.5 broadcast.1
  45.5 3.4 %reduce = f32[8,36864]{1,0:T(8,128)S(1)} reduce(f32[8,1,36864]{2,1,0:T(1,128)S(1)} %all_to_all.41, f32[]{:T(128)} %broadcast.1), dimensions={1}, to_apply=%all_to_all.29.reduce_sub_computation | reduce | bytes 2359300 | tf_op jit(solution)/shard_map/all_to_all | solution.py:11
  49.0 3.7 %reshape.7 = f32[32,12,24,32]{3,2,1,0:T(8,128)} reshape(f32[8,36864]{1,0:T(8,128)S(1)} %reduce) | data formatting | bytes 2359296
  52.7 6.3 %copy.10 = f32[8,4,32,24,12]{3,0,2,4,1:T(8,128)} copy(f32[8,4,32,24,12]{2,3,4,1,0:T(8,128)} %bitcast.19) | data formatting | bytes 2359296 | tf_op jit(solution)/shard_map/all_to_all | solution.py:11
  59.0 4.3 %all_to_all.32 = f32[4,32,192,12]{2,1,3,0:T(8,128)S(1)} reshape(f32[4,32,8,24,12]{3,2,1,4,0:T(8,128)} %bitcast.18) | data formatting | bytes 2359296 | tf_op jit(solution)/shard_map/all_to_all | solution.py:11
  63.3 1.0 copy.11
  64.3 49.3 %all_to_all.42 = f32[4,32,192,12]{2,0,3,1:T(4,128)S(1)} all-to-all(f32[4,32,192,12]{2,0,3,1:T(4,128)S(1)} %copy.11), channel_id=1, replica_groups=mesh['row'=8,'col'=16] {'col'}, dimensions={1} | all-to-all | bytes 2359296 | tf_op jit(solution)/shard_map/all_to_all | solution.py:10
  113.7 1.2 copy.12
  114.9 1.0 copy.13
  115.9 1.2 stack_reshape.2
  117.1 0.6 stack.3
  117.8 125.6 %all_to_all.43 = f32[8,768,384]{2,1,0:T(8,128)} all-to-all(f32[8,768,384]{2,1,0:T(8,128)S(1)} %stack.3), channel_id=1, replica_groups=mesh['row'=8,'col'=16] {'row'}, dimensions={0} | all-to-all | bytes 18874368 | tf_op jit(solution)/shard_map/all_to_all | solution.py:21
  243.4 0.0 all-gather.2.cloned.1.call-done
  243.4 34.1 %fusion = f32[768,384]{1,0:T(8,128)} fusion(f32[768,6144]{1,0:T(8,128)} %all-gather.2.cloned.1.call-done, f32[6144,384]{1,0:T(8,128)} %bitcast.17), kind=kOutput, calls=%fused_computation | convolution fusion | flops 21743271936 | bytes 29491200 | tf_op jit(solution)/shard_map/dot_general | solution.py:22
Async XLA Ops:
  6.5 236.8 %all-gather.2.cloned.1.call-start = ((), (), s32[]{:S(2)}) async-start(), calls=%async_computation.3 | async-start | bytes 20054016 | tf_op jit(solution)/shard_map/all_gather | solution.py:23
Sparse Core Ops, SparseCore 0:
  9.0 148.4 all-gather.1
